TPU v7x, 512 devices: a whole 4x4x16 slice. The times are simulated.
512 devices in a mesh: inst: 16 (over y_lo, x, core), sector: 32 (over y_hi, z).
Axes of the slice: x: 4, y: 4 (y_hi: 2, y_lo: 2; y = y_hi * 2 + y_lo), z: 16, core: 2. Of those that a mesh axis runs over, the one named last changes fastest.
Arguments:
- lam_init: float32 [16, 512, 32, 128], P('inst', 'sector'), may hold values from -6 to 6
- rhs: float32 [16, 512, 32, 128], P('inst', 'sector'), may hold values from -6 to 6
- relax: float32 [16, 512, 128], P('inst', 'sector'), may hold values from 0.15 to 0.6
- cond: float32 [512, 128], P('sector'), may hold values from 0.05 to 0.4
- jac: bfloat16 [16, 512, 6, 128, 128], P('inst', 'sector'), may hold values from -0.21875 to 0.21875
- rotor_jac: bfloat16 [16, 128, 128, 128], P('inst', 'sector'), may hold values from -0.5 to 0.5
- cols: int32 [512, 6], P('sector'), may hold values from 0 to 17
- rotor_shift: int32 [16, 128], P('inst', 'sector'), may hold values from 0 to 1
- owned: int32 [32], P('sector'), may hold values from 1 to 12, 288 in all
Outputs:
- adjoint: float32 [16, 512, 32, 128], P('inst', 'sector')
All inputs are finite; a program needn't handle non-finite values. No bound on the sum of `owned` on one device may be relied on, other than what follows from the above.
Results may differ from a plain program's by a relative error of at most 0.002.
Values may be sent and summed in bfloat16 or wider, within the bound.
No kernel may reach another device: no remote copies, remote signals or barrier semaphores. Data moves between devices by JAX's collectives and lax.ppermute only.
A program may use at most 64 MiB of HBM per device.

v0:
```python
import jax
import jax.numpy as jnp
from jax import lax
from jax.sharding import PartitionSpec as P

NT = 16
SWEEPS = 2


def padded(cells, sides, width):
    for axis, dim in sides:
        count = lax.axis_size(axis)
        head = lax.slice_in_dim(cells, 0, width, axis=dim)
        tail = lax.slice_in_dim(cells, cells.shape[dim] - width, cells.shape[dim], axis=dim)
        cells = jnp.concatenate(
            [
                lax.ppermute(tail, axis, [(i, (i + 1) % count) for i in range(count)]),
                cells,
                lax.ppermute(head, axis, [((i + 1) % count, i) for i in range(count)]),
            ],
            axis=dim,
        )
    return cells


def shifted(block, axis, distance):
    devices = range(lax.axis_size(axis))
    route = [((i - distance) % len(devices), i) for i in devices]
    return lax.ppermute(block, axis, route)


def spectral_matrix():
    index = jnp.arange(NT)
    offset = index[:, None] - index[None, :]
    angle = jnp.pi * offset.astype(jnp.float32) / NT
    safe_sin = jnp.where(offset == 0, jnp.float32(1.0), jnp.sin(angle))
    parity = jnp.where(offset % 2 == 0, jnp.float32(1.0), jnp.float32(-1.0))
    deriv = jnp.where(offset == 0, jnp.float32(0.0), 0.5 * parity * jnp.cos(angle) / safe_sin)
    return deriv + jnp.float32(2.0) / NT


def shards(lam_init, rhs, relax, cond, jac, rotor_jac, cols, rotor_shift, owned):
    local_inst = lam_init.shape[0]
    rows = lam_init.shape[1]
    rotor_rows = rotor_jac.shape[1]
    dspec = spectral_matrix()
    first_inst = lax.axis_index("inst") * local_inst
    row = jnp.arange(rows)
    live = ((row >= rows - rotor_rows) | (row < owned[0])).astype(jnp.float32)[None, :, None, None]
    lam = lam_init * live
    moving = rotor_shift.astype(jnp.float32)[:, :, None, None]
    relax_wide = relax[:, :, None, :]
    cond_wide = cond[None, :, None, :]
    for sweep in range(SWEEPS):
        lam_b = lam.astype(jnp.bfloat16)
        lam_h = padded(lam_b, (("sector", 1),), 1)
        picked = lam_h[:, cols]
        stator = jnp.einsum("tnkri,tnkio->tnro", picked, jac, preferred_element_type=jnp.float32)
        records = jnp.einsum(
            "tjri,tjio->tjro",
            lam_b[:, rows - rotor_rows :],
            rotor_jac,
            preferred_element_type=jnp.float32,
        )
        arrived = shifted((records * moving).astype(jnp.bfloat16), "sector", 1).astype(jnp.float32)
        rotor = records * (1.0 - moving) + arrived
        rotor_full = jnp.concatenate(
            [jnp.zeros((local_inst, rows - rotor_rows) + rotor.shape[2:], jnp.float32), rotor],
            axis=1,
        )
        weighted = lam * cond_wide
        piece = lax.all_gather(weighted, "inst", axis=0, tiled=True)
        coef = lax.dynamic_slice(dspec, (0, first_inst), (piece.shape[0], local_inst))
        spec = jnp.zeros_like(weighted) + jnp.einsum(
            "jt,jnrc->tnrc", coef, piece, precision=lax.Precision.HIGHEST
        )
        resid = rhs - (stator + rotor_full + spec)
        lam = lam + relax_wide * resid * live
    return lam


def solution(mesh):
    return jax.shard_map(
        shards,
        mesh=mesh,
        in_specs=(
            P("inst", "sector", None, None),
            P("inst", "sector", None, None),
            P("inst", "sector", None),
            P("sector", None),
            P("inst", "sector", None, None, None),
            P("inst", "sector", None, None),
            P("sector", None),
            P("inst", "sector"),
            P("sector"),
        ),
        out_specs=P("inst", "sector", None, None),
        check_vma=False,
    )
```

profile of v0, /device:TPU:1, one launch (start us, length us, event | category | flops | bytes accessed | tf_op | source)
XLA Modules:
  0.0 128.8 jit_solution(6784059207675336559)
XLA Ops:
  7.4 1.9 %multiply_convert_fusion = (bf16[1,16,32,128]{3,2,1,0:T(8,128)(2,1)S(1)}, f32[1,16,32,128]{3,2,1,0:T(8,128)}) fusion(f32[1,16,32,128]{3,2,1,0:T(8,128)} %param.9, f32[16]{0:T(128)S(1)} %or_convert_fusion, f32[16,128]{1,0:T(8,128)} %param.12), kind=kLoop, calls=%fused_computation.15 | loop fusion | flops 196608 | bytes 663616 | tf_op jit(solution)/shard_map/convert_element_type | solution.py:55
  9.3 0.7 convert_bitcast_fusion
  10.0 1.1 fusion.16
  11.1 0.7 fusion.18
  11.7 4.4 %collective-permute-start.2 = (bf16[1,4,32,128]{3,2,1,0:T(8,128)(2,1)}, bf16[1,4,32,128]{3,2,1,0:T(8,128)(2,1)S(1)}, u32[]{:S(2)}, u32[]{:S(2)}) collective-permute-start(bf16[1,4,32,128]{3,2,1,0:T(8,128)(2,1)} %fusion.18), channel_id=1, source_target_pairs={{31,0},{0,1},{1,2},{2,3},{3,4},{4,5},{5,6},{6,7},{7,8},{8,9},{9,10... | collective-permute-start | bytes 98312 | tf_op jit(solution)/shard_map/ppermute | solution.py:29
  16.1 12.1 %collective-permute-start.1 = (bf16[1,1,32,128]{3,2,1,0:T(8,128)(2,1)S(1)}, bf16[1,1,32,128]{3,2,1,0:T(8,128)(2,1)S(1)}, u32[]{:S(2)}, u32[]{:S(2)}) collective-permute-start(bf16[1,1,32,128]{3,2,1,0:T(8,128)(2,1)S(1)} %get-tuple-element.12), channel_id=1, source_target_pairs={{1,0},{2,1},{3,2},{4,3},{5,4},{6,5},{7,6},{8,7},{9,8},{10,9},{11,1... | collective-permute-start | bytes 24584 | tf_op jit(solution)/shard_map/ppermute | solution.py:19
  28.3 1.9 %collective-permute-start = (bf16[1,1,32,128]{3,2,1,0:T(8,128)(2,1)S(1)}, bf16[1,1,32,128]{3,2,1,0:T(8,128)(2,1)}, u32[]{:S(2)}, u32[]{:S(2)}) collective-permute-start(bf16[1,1,32,128]{3,2,1,0:T(8,128)(2,1)S(1)} %get-tuple-element.11), channel_id=1, source_target_pairs={{0,1},{1,2},{2,3},{3,4},{4,5},{5,6},{6,7},{7,8},{8,9},{9,10},{10,1... | collective-permute-start | bytes 24584 | tf_op jit(solution)/shard_map/ppermute | solution.py:17
  30.2 0.7 compare_select_fusion
  31.0 0.1 reshape.75
  31.1 1.2 broadcast_subtract_fusion
  32.3 0.6 copy-done.15
  32.9 3.6 %collective-permute-done = bf16[1,1,32,128]{3,2,1,0:T(8,128)(2,1)} collective-permute-done((bf16[1,1,32,128]{3,2,1,0:T(8,128)(2,1)S(1)}, bf16[1,1,32,128]{3,2,1,0:T(8,128)(2,1)}, u32[]{:S(2)}, u32[]{:S(2)}) %collective-permute-start) | collective-permute-done | bytes 8224 | tf_op jit(solution)/shard_map/ppermute | solution.py:17
  36.5 0.7 maximum_bitcast_fusion
  37.2 1.6 %gather_fusion = bf16[96,32,128]{2,1,0:T(8,128)(2,1)} fusion(bf16[18,32,128]{2,1,0:T(8,128)(2,1)S(1)} %maximum_bitcast_fusion, s32[1024]{0:T(1024)S(1)} %pad_clamp_fusion), kind=kCustom, calls=%fused_computation | custom fusion | bytes 1573248 | tf_op jit(solution)/shard_map/gather | solution.py:57
  38.8 1.3 %bitcast_add_fusion.1 = f32[1,4,32,128]{3,2,1,0:T(8,128)} fusion(bf16[1,4,32,128]{3,2,1,0:T(8,128)(2,1)S(1)} %collective-permute-done.2, f32[4,32,128]{2,1,0:T(8,128)S(1)} %fusion.16, f32[4]{0:T(128)} %broadcast_subtract_fusion), kind=kLoop, calls=%fused_computation.24 | loop fusion | flops 49152 | bytes 163856 | tf_op jit(solution)/shard_map/add | solution.py:66
  40.1 20.2 %all-gather.3.cloned.1.call-done = f32[16,16,32,128]{3,2,1,0:T(8,128)} async-done(((f32[1,16,32,128]{3,2,1,0:T(8,128)}), f32[16,16,32,128]{3,2,1,0:T(8,128)}) %all-gather.3.cloned.1.call-update) | async-done | bytes 4194320 | tf_op jit(solution)/shard_map/all_gather | solution.py:72
  60.4 6.5 %fusion.2 = f32[1,16,32,128]{3,0,2,1:T(1,128)S(1)} fusion(f32[16,16,32,128]{3,2,1,0:T(8,128)} %all-gather.3.cloned.1.call-done, f32[16,16]{0,1:T(8,128)S(1)} %get-tuple-element.14, s32[]{:T(128)S(6)} %select_n.31, pred[16,16]{0,1:T(8,128)(4,1)S(1)} %fusion.21, s32[16,16]{0,1:T(8,128)S(1)} %get-tuple-element.13), kind=kOutput, calls=%fused_computation.4 | convolution fusion | flops 12583056 | bytes 4457988 | tf_op jit(solution)/shard_map/jt,jnrc->tnrc/dot_general | solution.py:74
  67.0 0.7 fusion.32
  67.7 0.7 broadcast_multiply_fusion
  68.5 7.7 %collective-permute-start.4 = (bf16[1,1,32,128]{3,2,1,0:T(8,128)(2,1)S(1)}, bf16[1,1,32,128]{3,2,1,0:T(8,128)(2,1)S(1)}, u32[]{:S(2)}, u32[]{:S(2)}) collective-permute-start(bf16[1,1,32,128]{3,2,1,0:T(8,128)(2,1)S(1)} %get-tuple-element.10), channel_id=1, source_target_pairs={{1,0},{2,1},{3,2},{4,3},{5,4},{6,5},{7,6},{8,7},{9,8},{10,9},{11,1... | collective-permute-start | bytes 24584 | tf_op jit(solution)/shard_map/ppermute | solution.py:19
  76.3 1.9 %collective-permute-start.3 = (bf16[1,1,32,128]{3,2,1,0:T(8,128)(2,1)S(1)}, bf16[1,1,32,128]{3,2,1,0:T(8,128)(2,1)S(1)}, u32[]{:S(2)}, u32[]{:S(2)}) collective-permute-start(bf16[1,1,32,128]{3,2,1,0:T(8,128)(2,1)S(1)} %get-tuple-element.9), channel_id=1, source_target_pairs={{0,1},{1,2},{2,3},{3,4},{4,5},{5,6},{6,7},{7,8},{8,9},{9,10},{10,1... | collective-permute-start | bytes 24584 | tf_op jit(solution)/shard_map/ppermute | solution.py:17
  78.2 1.1 fusion.14
  79.2 1.4 %fusion.19 = bf16[1,4,32,128]{3,2,1,0:T(8,128)(2,1)} fusion(f32[4,32,128]{2,1,0:T(8,128)S(1)} %fusion.14, f32[4]{0:T(128)} %copy-done.20), kind=kLoop, calls=%fused_computation.28 | loop fusion | flops 32768 | bytes 98320 | tf_op jit(solution)/shard_map/convert_element_type | solution.py:65
  80.6 1.9 %collective-permute-start.5 = (bf16[1,4,32,128]{3,2,1,0:T(8,128)(2,1)}, bf16[1,4,32,128]{3,2,1,0:T(8,128)(2,1)}, u32[]{:S(2)}, u32[]{:S(2)}) collective-permute-start(bf16[1,4,32,128]{3,2,1,0:T(8,128)(2,1)} %fusion.19), channel_id=1, source_target_pairs={{31,0},{0,1},{1,2},{2,3},{3,4},{4,5},{5,6},{6,7},{7,8},{8,9},{9,10... | collective-permute-start | bytes 98312 | tf_op jit(solution)/shard_map/ppermute | solution.py:29
  82.5 1.7 %collective-permute-done.3 = bf16[1,1,32,128]{3,2,1,0:T(8,128)(2,1)S(1)} collective-permute-done((bf16[1,1,32,128]{3,2,1,0:T(8,128)(2,1)S(1)}, bf16[1,1,32,128]{3,2,1,0:T(8,128)(2,1)S(1)}, u32[]{:S(2)}, u32[]{:S(2)}) %collective-permute-start.3) | collective-permute-done | bytes 8224 | tf_op jit(solution)/shard_map/ppermute | solution.py:17
  84.3 0.9 maximum_bitcast_fusion.1
  85.2 1.7 %gather_fusion.1 = bf16[96,32,128]{2,1,0:T(8,128)(2,1)} fusion(bf16[18,32,128]{2,1,0:T(8,128)(2,1)S(1)} %maximum_bitcast_fusion.1, s32[1024]{0:T(1024)} %copy-done.9), kind=kCustom, calls=%fused_computation.1 | custom fusion | bytes 1573248 | tf_op jit(solution)/shard_map/gather | solution.py:57
  86.9 2.4 %collective-permute-done.5 = bf16[1,4,32,128]{3,2,1,0:T(8,128)(2,1)} collective-permute-done((bf16[1,4,32,128]{3,2,1,0:T(8,128)(2,1)}, bf16[1,4,32,128]{3,2,1,0:T(8,128)(2,1)}, u32[]{:S(2)}, u32[]{:S(2)}) %collective-permute-start.5) | collective-permute-done | bytes 32800 | tf_op jit(solution)/shard_map/ppermute | solution.py:29
  89.3 0.9 bitcast_add_fusion
  90.2 23.8 %all-gather.5.cloned.1.call-done = f32[16,16,32,128]{3,2,1,0:T(8,128)} async-done(((f32[1,16,32,128]{3,2,1,0:T(8,128)}), f32[16,16,32,128]{3,2,1,0:T(8,128)}) %all-gather.5.cloned.1.call-update) | async-done | bytes 4194320 | tf_op jit(solution)/shard_map/all_gather | solution.py:72
  114.0 6.5 %fusion = f32[1,16,32,128]{3,0,2,1:T(1,128)S(1)} fusion(f32[16,16,32,128]{3,2,1,0:T(8,128)} %all-gather.5.cloned.1.call-done, f32[16,16]{0,1:T(8,128)} %copy-done.14, s32[]{:T(128)S(6)} %select_n.31, pred[16,16]{0,1:T(8,128)(4,1)} %copy-done.16, s32[16,16]{0,1:T(8,128)} %copy-done.13), kind=kOutput, calls=%fused_computation.2 | convolution fusion | flops 12583056 | bytes 4457988 | tf_op jit(solution)/shard_map/jt,jnrc->tnrc/dot_general | solution.py:74
  120.5 1.4 %multiply_add_fusion = f32[1,16,32,128]{3,2,1,0:T(8,128)} fusion(f32[1,16,32,128]{3,2,1,0:T(8,128)S(1)} %get-tuple-element.6, f32[1,16,32,128]{3,2,1,0:T(8,128)S(1)} %copy-done.5, f32[1,16,32,128]{3,2,1,0:T(8,128)S(1)} %bitcast.74, f32[1,4,32,128]{3,2,1,0:T(8,128)S(1)} %bitcast_add_fusion, f32[16,128]{1,0:T(8,128)S(1)} %bitcast.77, f32[16]{0:T(128)S(1)} %copy-done.19, ...), kind=kOutput, calls=%fused_computation.12 | convolution fusion | flops 101056512 | bytes 5054528 | tf_op jit(solution)/shard_map/tnkri,tnkio->tnro/dot_general | solution.py:58
  (55 shorter events, 0.3 us)
Async XLA Ops:
  6.5 60.4 %copy-start = (bf16[1,16,6,128,128]{4,3,2,1,0:T(8,128)(2,1)S(1)}, bf16[1,16,6,128,128]{4,3,2,1,0:T(8,128)(2,1)}, u32[]{:S(2)}) copy-start(bf16[1,16,6,128,128]{4,3,2,1,0:T(8,128)(2,1)} %param.13) | copy-start | bytes 9437188
  6.5 60.4 %copy-start.11 = (f32[1,16,128]{2,1,0:T(8,128)S(1)}, f32[1,16,128]{2,1,0:T(8,128)}, u32[]{:S(2)}) copy-start(f32[1,16,128]{2,1,0:T(8,128)} %param.11) | copy-start | bytes 24580
  6.5 53.8 %all-gather.3.cloned.1.call-start = ((), (), s32[]{:S(2)}) async-start(), calls=%async_computation | async-start | bytes 4456448 | tf_op jit(solution)/shard_map/all_gather | solution.py:72
  7.4 2.7 %copy-start.17 = (f32[16]{0:T(128)}, f32[16]{0:T(128)S(1)}, u32[]{:S(2)}) copy-start(f32[16]{0:T(128)S(1)} %or_convert_fusion) | copy-start | bytes 196
  9.3 104.7 %all-gather.5.cloned.1.call-start = ((), (), s32[]{:S(2)}) async-start(), calls=%async_computation.1 | async-start | bytes 4456448 | tf_op jit(solution)/shard_map/all_gather | solution.py:72
  10.0 6.1 %copy-start.20 = (f32[4]{0:T(128)}, f32[4]{0:T(128)S(1)}, u32[]{:S(2)}) copy-start(f32[4]{0:T(128)S(1)} %convert_bitcast_fusion) | copy-start | bytes 52
  11.7 27.1 %collective-permute-start.2 = (bf16[1,4,32,128]{3,2,1,0:T(8,128)(2,1)}, bf16[1,4,32,128]{3,2,1,0:T(8,128)(2,1)S(1)}, u32[]{:S(2)}, u32[]{:S(2)}) collective-permute-start(bf16[1,4,32,128]{3,2,1,0:T(8,128)(2,1)} %fusion.18), channel_id=1, source_target_pairs={{31,0},{0,1},{1,2},{2,3},{3,4},{4,5},{5,6},{6,7},{7,8},{8,9},{9,10... | collective-permute-start | bytes 98312 | tf_op jit(solution)/shard_map/ppermute | solution.py:29
  16.1 16.2 %collective-permute-start.1 = (bf16[1,1,32,128]{3,2,1,0:T(8,128)(2,1)S(1)}, bf16[1,1,32,128]{3,2,1,0:T(8,128)(2,1)S(1)}, u32[]{:S(2)}, u32[]{:S(2)}) collective-permute-start(bf16[1,1,32,128]{3,2,1,0:T(8,128)(2,1)S(1)} %get-tuple-element.12), channel_id=1, source_target_pairs={{1,0},{2,1},{3,2},{4,3},{5,4},{6,5},{7,6},{8,7},{9,8},{10,9},{11,1... | collective-permute-start | bytes 24584 | tf_op jit(solution)/shard_map/ppermute | solution.py:19
  28.3 8.2 %collective-permute-start = (bf16[1,1,32,128]{3,2,1,0:T(8,128)(2,1)S(1)}, bf16[1,1,32,128]{3,2,1,0:T(8,128)(2,1)}, u32[]{:S(2)}, u32[]{:S(2)}) collective-permute-start(bf16[1,1,32,128]{3,2,1,0:T(8,128)(2,1)S(1)} %get-tuple-element.11), channel_id=1, source_target_pairs={{0,1},{1,2},{2,3},{3,4},{4,5},{5,6},{6,7},{7,8},{8,9},{9,10},{10,1... | collective-permute-start | bytes 24584 | tf_op jit(solution)/shard_map/ppermute | solution.py:17
  31.1 35.9 %copy-start.9 = (s32[1024]{0:T(1024)}, s32[1024]{0:T(1024)S(1)}, u32[]{:S(2)}) copy-start(s32[1024]{0:T(1024)S(1)} %pad_clamp_fusion) | copy-start | bytes 12292
  31.1 35.8 %copy-start.13 = (s32[16,16]{0,1:T(8,128)}, s32[16,16]{0,1:T(8,128)S(1)}, u32[]{:S(2)}) copy-start(s32[16,16]{0,1:T(8,128)S(1)} %get-tuple-element.13) | copy-start | bytes 3076
  31.1 36.6 %copy-start.14 = (f32[16,16]{0,1:T(8,128)}, f32[16,16]{0,1:T(8,128)S(1)}, u32[]{:S(2)}) copy-start(f32[16,16]{0,1:T(8,128)S(1)} %get-tuple-element.14) | copy-start | bytes 3076
  32.3 34.7 %copy-start.16 = (pred[16,16]{0,1:T(8,128)(4,1)}, pred[16,16]{0,1:T(8,128)(4,1)S(1)}, u32[]{:S(2)}) copy-start(pred[16,16]{0,1:T(8,128)(4,1)S(1)} %fusion.21) | copy-start | bytes 772
  32.3 0.6 copy-start.15
  60.4 6.6 %copy-start.2 = (bf16[96,32,128]{2,1,0:T(8,128)(2,1)S(1)}, bf16[96,32,128]{2,1,0:T(8,128)(2,1)}, u32[]{:S(2)}) copy-start(bf16[96,32,128]{2,1,0:T(8,128)(2,1)} %gather_fusion) | copy-start | bytes 2359300
  60.4 6.6 %copy-start.3 = (f32[1,16,32,128]{3,2,1,0:T(8,128)S(1)}, f32[1,16,32,128]{3,2,1,0:T(8,128)}, u32[]{:S(2)}) copy-start(f32[1,16,32,128]{3,2,1,0:T(8,128)} %param.9) | copy-start | bytes 786436
  60.4 6.6 %copy-start.4 = (f32[1,16,32,128]{3,2,1,0:T(8,128)S(1)}, f32[1,16,32,128]{3,2,1,0:T(8,128)}, u32[]{:S(2)}) copy-start(f32[1,16,32,128]{3,2,1,0:T(8,128)} %param.10) | copy-start | bytes 786436
  60.4 6.7 %copy-start.8 = (f32[1,4,32,128]{3,2,1,0:T(8,128)S(1)}, f32[1,4,32,128]{3,2,1,0:T(8,128)}, u32[]{:S(2)}) copy-start(f32[1,4,32,128]{3,2,1,0:T(8,128)} %bitcast_add_fusion.1) | copy-start | bytes 196612
  60.4 6.7 %copy-start.18 = (f32[16]{0:T(128)S(1)}, f32[16]{0:T(128)}, u32[]{:S(2)}) copy-start(f32[16]{0:T(128)} %copy-done.17) | copy-start | bytes 196
  60.4 7.4 %copy-start.10 = (f32[16,128]{1,0:T(8,128)S(1)}, f32[16,128]{1,0:T(8,128)}, u32[]{:S(2)}) copy-start(f32[16,128]{1,0:T(8,128)} %param.12) | copy-start | bytes 24580
  67.7 14.8 %copy-start.6 = (bf16[1,16,32,128]{3,2,1,0:T(8,128)(2,1)}, bf16[1,16,32,128]{3,2,1,0:T(8,128)(2,1)S(1)}, u32[]{:S(2)}) copy-start(bf16[1,16,32,128]{3,2,1,0:T(8,128)(2,1)S(1)} %get-tuple-element.5) | copy-start | bytes 393220
  68.5 14.0 %collective-permute-start.4 = (bf16[1,1,32,128]{3,2,1,0:T(8,128)(2,1)S(1)}, bf16[1,1,32,128]{3,2,1,0:T(8,128)(2,1)S(1)}, u32[]{:S(2)}, u32[]{:S(2)}) collective-permute-start(bf16[1,1,32,128]{3,2,1,0:T(8,128)(2,1)S(1)} %get-tuple-element.10), channel_id=1, source_target_pairs={{1,0},{2,1},{3,2},{4,3},{5,4},{6,5},{7,6},{8,7},{9,8},{10,9},{11,1... | collective-permute-start | bytes 24584 | tf_op jit(solution)/shard_map/ppermute | solution.py:19
  76.3 8.0 %collective-permute-start.3 = (bf16[1,1,32,128]{3,2,1,0:T(8,128)(2,1)S(1)}, bf16[1,1,32,128]{3,2,1,0:T(8,128)(2,1)S(1)}, u32[]{:S(2)}, u32[]{:S(2)}) collective-permute-start(bf16[1,1,32,128]{3,2,1,0:T(8,128)(2,1)S(1)} %get-tuple-element.9), channel_id=1, source_target_pairs={{0,1},{1,2},{2,3},{3,4},{4,5},{5,6},{6,7},{7,8},{8,9},{9,10},{10,1... | collective-permute-start | bytes 24584 | tf_op jit(solution)/shard_map/ppermute | solution.py:17
  79.2 5.0 %copy-start.7 = (f32[4,32,128]{2,1,0:T(8,128)}, f32[4,32,128]{2,1,0:T(8,128)S(1)}, u32[]{:S(2)}) copy-start(f32[4,32,128]{2,1,0:T(8,128)S(1)} %fusion.14) | copy-start | bytes 196612
  80.6 8.7 %collective-permute-start.5 = (bf16[1,4,32,128]{3,2,1,0:T(8,128)(2,1)}, bf16[1,4,32,128]{3,2,1,0:T(8,128)(2,1)}, u32[]{:S(2)}, u32[]{:S(2)}) collective-permute-start(bf16[1,4,32,128]{3,2,1,0:T(8,128)(2,1)} %fusion.19), channel_id=1, source_target_pairs={{31,0},{0,1},{1,2},{2,3},{3,4},{4,5},{5,6},{6,7},{7,8},{8,9},{9,10... | collective-permute-start | bytes 98312 | tf_op jit(solution)/shard_map/ppermute | solution.py:29
  86.9 33.6 %copy-start.12 = (f32[1,16,128]{2,1,0:T(8,128)S(1)}, f32[1,16,128]{2,1,0:T(8,128)}, u32[]{:S(2)}) copy-start(f32[1,16,128]{2,1,0:T(8,128)} %param.11) | copy-start | bytes 24580
  86.9 33.6 %copy-start.19 = (f32[16]{0:T(128)S(1)}, f32[16]{0:T(128)}, u32[]{:S(2)}) copy-start(f32[16]{0:T(128)} %copy-done.17) | copy-start | bytes 196
  114.0 6.6 %copy-start.1 = (bf16[96,32,128]{2,1,0:T(8,128)(2,1)S(1)}, bf16[96,32,128]{2,1,0:T(8,128)(2,1)}, u32[]{:S(2)}) copy-start(bf16[96,32,128]{2,1,0:T(8,128)(2,1)} %gather_fusion.1) | copy-start | bytes 2359300
  114.0 6.6 %copy-start.5 = (f32[1,16,32,128]{3,2,1,0:T(8,128)S(1)}, f32[1,16,32,128]{3,2,1,0:T(8,128)}, u32[]{:S(2)}) copy-start(f32[1,16,32,128]{3,2,1,0:T(8,128)} %param.10) | copy-start | bytes 786436
Sparse Core Ops, SparseCore 0:
  9.5 50.8 all-gather.2
  68.6 45.2 all-gather.4
where the time goes:
time: 129 us
  waiting for transfers between devices  51.7 us (40%)
  starting transfers between devices  30 us (23%)
  matrix products  17.2 us (13%)
  between operations  14.6 us (11%)
  other arithmetic  11.1 us (9%)
  local copies, waits for them, and re-layouts  4.14 us (3%)
    all_gather x2, waiting for transfers between devices, shards(): piece = lax.all_gather(weighted, 'inst', axis=0, tiled=True)  44 us
    ppermute x2, starting transfers between devices, padded(): lax.ppermute(head, axis, [((i + 1) % count, i) for i in range(count)])  19.9 us
    dot_general x2, matrix products, shards(): jnp.einsum('jt,jnrc->tnrc', coef, piece, precision=lax.Precision.HIGHEST)  13.1 us
    ppermute x2, starting transfers between devices, shifted(): return lax.ppermute(block, axis, route)  6.27 us
    ppermute x2, waiting for transfers between devices, padded(): lax.ppermute(tail, axis, [(i, (i + 1) % count) for i in range(count)])  5.31 us
    ppermute x2, starting transfers between devices, padded(): lax.ppermute(tail, axis, [(i, (i + 1) % count) for i in range(count)])  3.84 us
    gather x2, local copies, waits for them, and re-layouts, shards(): picked = lam_h[:, cols]  3.29 us
  transfers between devices with their start and end apart: 8, of which 5 were waited for; matrix products, arithmetic and copies ran while one was open for 11% of the time, Pallas kernels for 0%

commit v1 on v0

--- a/solution.py
+++ b/solution.py
@@ -69,7 +69,9 @@
             axis=1,
         )
         weighted = lam * cond_wide
-        piece = lax.all_gather(weighted, "inst", axis=0, tiled=True)
+        piece = jnp.concatenate(
+            lax.all_to_all(jnp.stack([weighted] * lax.axis_size("inst")), "inst", 0, 0), axis=0
+        )
         coef = lax.dynamic_slice(dspec, (0, first_inst), (piece.shape[0], local_inst))
         spec = jnp.zeros_like(weighted) + jnp.einsum(
             "jt,jnrc->tnrc", coef, piece, precision=lax.Precision.HIGHEST

time: 129 us -> 155 us (1.20)
  waiting for transfers between devices: 51.7 us -> 76.2 us
  between operations: 14.6 us -> 1.2 us
  starting transfers between devices: 30 us -> 42.2 us
  local copies, waits for them, and re-layouts: 4.14 us -> 9.87 us
  other arithmetic: 11.1 us -> 7.06 us
    all_to_all x0 -> x2, waiting for transfers between devices: none -> 67.1 us  [shards(): lax.all_to_all(jnp.stack([weighted] * lax.axis_size('inst')), 'inst', 0, 0)]
    all_gather x2 -> x0, waiting for transfers between devices: 44 us -> none  [shards(): piece = lax.all_gather(weighted, 'inst', axis=0, tiled=True)]
    all_to_all x0 -> x2, starting transfers between devices: none -> 16.7 us  [shards(): lax.all_to_all(jnp.stack([weighted] * lax.axis_size('inst')), 'inst', 0, 0)]
    another operation x0 -> x2, local copies, waits for them, and re-layouts: none -> 5.13 us  [shards(): jnp.stack([weighted] * lax.axis_size('inst'))]
    ppermute x2, starting transfers between devices: 19.9 us -> 17.6 us  [padded(): lax.ppermute(head, axis, [((i + 1) % count, i) for i in range(count)])]
    ppermute x2, starting transfers between devices: 6.27 us -> 4 us  [shifted(): return lax.ppermute(block, axis, route)]
    ppermute x2, waiting for transfers between devices: 5.31 us -> 7.18 us  [padded(): lax.ppermute(tail, axis, [(i, (i + 1) % count) for i in range(count)])]
  transfers between devices with their start and end apart: 8 -> 8, of which waited for: 5 -> 5; matrix products, arithmetic and copies ran while one was open for 11% -> 7% of each run, Pallas kernels for 0% -> 0%
where the time goes in v1:
time: 155 us; the launch traced here: 154 us
  waiting for transfers between devices  76.2 us (49%)
  starting transfers between devices  42.2 us (27%)
  matrix products  17.3 us (11%)
  local copies, waits for them, and re-layouts  9.87 us (6%)
  other arithmetic  7.06 us (5%)
    all_to_all x2, waiting for transfers between devices, shards(): lax.all_to_all(jnp.stack([weighted] * lax.axis_size('inst')), 'inst', 0, 0)  67.1 us
    ppermute x2, starting transfers between devices, padded(): lax.ppermute(head, axis, [((i + 1) % count, i) for i in range(count)])  17.6 us
    all_to_all x2, starting transfers between devices, shards(): lax.all_to_all(jnp.stack([weighted] * lax.axis_size('inst')), 'inst', 0, 0)  16.7 us
    dot_general x2, matrix products, shards(): jnp.einsum('jt,jnrc->tnrc', coef, piece, precision=lax.Precision.HIGHEST)  13.1 us
    ppermute x2, waiting for transfers between devices, padded(): lax.ppermute(tail, axis, [(i, (i + 1) % count) for i in range(count)])  7.18 us
    another operation x2, local copies, waits for them, and re-layouts, shards(): jnp.stack([weighted] * lax.axis_size('inst'))  5.13 us
    ppermute x2, starting transfers between devices, shifted(): return lax.ppermute(block, axis, route)  4 us
    ppermute x2, starting transfers between devices, padded(): lax.ppermute(tail, axis, [(i, (i + 1) % count) for i in range(count)])  3.84 us
  transfers between devices with their start and end apart: 8, of which 5 were waited for; matrix products, arithmetic and copies ran while one was open for 7% of the time, Pallas kernels for 0%

profile of v1, /device:TPU:1, one launch (start us, length us, event | category | flops | bytes accessed | tf_op | source)
XLA Modules:
  0.0 153.8 jit_solution(2594864123116944374)
XLA Ops:
  0.8 0.5 copy-done.16
  1.3 1.1 multiply_convert_fusion
  2.4 2.6 %stack.4 = f32[16,1,16,32,128]{4,3,2,1,0:T(8,128)} broadcast(f32[16,32,128]{2,1,0:T(8,128)S(1)} %get-tuple-element.8), dimensions={2,3,4} | broadcast | bytes 4456448 | tf_op jit(solution)/shard_map/stack | solution.py:73
  5.0 11.3 %all-to-all-start = ((f32[16,1,16,32,128]{4,3,2,1,0:T(8,128)}), f32[16,1,16,32,128]{4,3,2,1,0:T(8,128)}, u32[]{:S(2)}, u32[]{:S(2)}) async-start(f32[16,1,16,32,128]{4,3,2,1,0:T(8,128)} %stack.4), calls=%async_computation | async-start | bytes 8388608 | tf_op jit(solution)/shard_map/all_to_all | solution.py:73
  16.4 0.7 fusion.18
  17.1 1.9 %collective-permute-start.2 = (bf16[1,4,32,128]{3,2,1,0:T(8,128)(2,1)}, bf16[1,4,32,128]{3,2,1,0:T(8,128)(2,1)S(1)}, u32[]{:S(2)}, u32[]{:S(2)}) collective-permute-start(bf16[1,4,32,128]{3,2,1,0:T(8,128)(2,1)} %fusion.18), channel_id=1, source_target_pairs={{31,0},{0,1},{1,2},{2,3},{3,4},{4,5},{5,6},{6,7},{7,8},{8,9},{9,10... | collective-permute-start | bytes 98312 | tf_op jit(solution)/shard_map/ppermute | solution.py:29
  19.1 9.1 %collective-permute-start.1 = (bf16[1,1,32,128]{3,2,1,0:T(8,128)(2,1)S(1)}, bf16[1,1,32,128]{3,2,1,0:T(8,128)(2,1)S(1)}, u32[]{:S(2)}, u32[]{:S(2)}) collective-permute-start(bf16[1,1,32,128]{3,2,1,0:T(8,128)(2,1)S(1)} %get-tuple-element.12), channel_id=1, source_target_pairs={{1,0},{2,1},{3,2},{4,3},{5,4},{6,5},{7,6},{8,7},{9,8},{10,9},{11,1... | collective-permute-start | bytes 24584 | tf_op jit(solution)/shard_map/ppermute | solution.py:19
  28.2 1.9 %collective-permute-start = (bf16[1,1,32,128]{3,2,1,0:T(8,128)(2,1)S(1)}, bf16[1,1,32,128]{3,2,1,0:T(8,128)(2,1)}, u32[]{:S(2)}, u32[]{:S(2)}) collective-permute-start(bf16[1,1,32,128]{3,2,1,0:T(8,128)(2,1)S(1)} %get-tuple-element.11), channel_id=1, source_target_pairs={{0,1},{1,2},{2,3},{3,4},{4,5},{5,6},{6,7},{7,8},{8,9},{9,10},{10,1... | collective-permute-start | bytes 24584 | tf_op jit(solution)/shard_map/ppermute | solution.py:17
  30.4 0.6 broadcast_subtract_fusion
  31.0 0.6 copy-done.14
  31.6 4.9 %collective-permute-done = bf16[1,1,32,128]{3,2,1,0:T(8,128)(2,1)} collective-permute-done((bf16[1,1,32,128]{3,2,1,0:T(8,128)(2,1)S(1)}, bf16[1,1,32,128]{3,2,1,0:T(8,128)(2,1)}, u32[]{:S(2)}, u32[]{:S(2)}) %collective-permute-start) | collective-permute-done | bytes 8224 | tf_op jit(solution)/shard_map/ppermute | solution.py:17
  36.5 0.7 maximum_bitcast_fusion
  37.2 1.6 %gather_fusion = bf16[96,32,128]{2,1,0:T(8,128)(2,1)} fusion(bf16[18,32,128]{2,1,0:T(8,128)(2,1)S(1)} %maximum_bitcast_fusion, s32[1024]{0:T(1024)S(1)} %pad_clamp_fusion), kind=kCustom, calls=%fused_computation | custom fusion | bytes 1573248 | tf_op jit(solution)/shard_map/gather | solution.py:57
  38.9 1.4 bitcast_add_fusion.1
  40.3 32.6 %all-to-all-done = f32[16,1,16,32,128]{4,3,2,1,0:T(8,128)} async-done(((f32[16,1,16,32,128]{4,3,2,1,0:T(8,128)}), f32[16,1,16,32,128]{4,3,2,1,0:T(8,128)}, u32[]{:S(2)}, u32[]{:S(2)}) %all-to-all-start) | async-done | bytes 4194336 | tf_op jit(solution)/shard_map/all_to_all | solution.py:73
  72.8 6.5 %fusion.2 = f32[1,16,32,128]{3,0,2,1:T(1,128)S(1)} fusion(f32[16,16,32,128]{3,2,1,0:T(8,128)} %bitcast.17, f32[16,16]{0,1:T(8,128)S(1)} %get-tuple-element.14, s32[]{:T(128)S(6)} %select_n.31, pred[16,16]{0,1:T(8,128)(4,1)S(1)} %fusion.21, s32[16,16]{0,1:T(8,128)S(1)} %get-tuple-element.13), kind=kOutput, calls=%fused_computation.4 | convolution fusion | flops 12583056 | bytes 4457988 | tf_op jit(solution)/shard_map/jt,jnrc->tnrc/dot_general | solution.py:76
  79.4 1.7 %fusion.32 = (bf16[1,16,32,128]{3,2,1,0:T(8,128)(2,1)S(1)}, f32[1,16,32,128]{3,2,1,0:T(8,128)S(1)}) fusion(f32[1,16,32,128]{3,2,1,0:T(8,128)} %param.10, f32[1,16,32,128]{3,2,1,0:T(8,128)S(1)} %bitcast.81, f32[1,4,32,128]{3,2,1,0:T(8,128)S(1)} %copy-done.7, f32[16,128]{1,0:T(8,128)S(1)} %bitcast.82, f32[1,16,32,128]{3,2,1,0:T(8,128)} %param.9, ...), kind=kOutput, calls=%fused_computation.55 | convolution fusion | flops 101187584 | bytes 5185600 | tf_op jit(solution)/shard_map/tnkri,tnkio->tnro/dot_general | solution.py:58
  81.2 2.6 %stack.5 = f32[16,1,16,32,128]{4,3,2,1,0:T(8,128)} broadcast(f32[16,32,128]{2,1,0:T(8,128)S(1)} %multiply_bitcast_fusion), dimensions={2,3,4} | broadcast | bytes 4456448 | tf_op jit(solution)/shard_map/stack | solution.py:73
  83.8 5.5 %all-to-all-start.1 = ((f32[16,1,16,32,128]{4,3,2,1,0:T(8,128)}), f32[16,1,16,32,128]{4,3,2,1,0:T(8,128)}, u32[]{:S(2)}, u32[]{:S(2)}) async-start(f32[16,1,16,32,128]{4,3,2,1,0:T(8,128)} %stack.5), calls=%async_computation.1 | async-start | bytes 8388608 | tf_op jit(solution)/shard_map/all_to_all | solution.py:73
  89.2 8.4 %collective-permute-start.4 = (bf16[1,1,32,128]{3,2,1,0:T(8,128)(2,1)S(1)}, bf16[1,1,32,128]{3,2,1,0:T(8,128)(2,1)S(1)}, u32[]{:S(2)}, u32[]{:S(2)}) collective-permute-start(bf16[1,1,32,128]{3,2,1,0:T(8,128)(2,1)S(1)} %get-tuple-element.10), channel_id=1, source_target_pairs={{1,0},{2,1},{3,2},{4,3},{5,4},{6,5},{7,6},{8,7},{9,8},{10,9},{11,1... | collective-permute-start | bytes 24584 | tf_op jit(solution)/shard_map/ppermute | solution.py:19
  97.7 1.9 %collective-permute-start.3 = (bf16[1,1,32,128]{3,2,1,0:T(8,128)(2,1)S(1)}, bf16[1,1,32,128]{3,2,1,0:T(8,128)(2,1)S(1)}, u32[]{:S(2)}, u32[]{:S(2)}) collective-permute-start(bf16[1,1,32,128]{3,2,1,0:T(8,128)(2,1)S(1)} %get-tuple-element.9), channel_id=1, source_target_pairs={{0,1},{1,2},{2,3},{3,4},{4,5},{5,6},{6,7},{7,8},{8,9},{9,10},{10,1... | collective-permute-start | bytes 24584 | tf_op jit(solution)/shard_map/ppermute | solution.py:17
  99.6 1.1 fusion.14
  100.7 0.7 fusion.19
  101.4 2.1 %collective-permute-start.5 = (bf16[1,4,32,128]{3,2,1,0:T(8,128)(2,1)}, bf16[1,4,32,128]{3,2,1,0:T(8,128)(2,1)}, u32[]{:S(2)}, u32[]{:S(2)}) collective-permute-start(bf16[1,4,32,128]{3,2,1,0:T(8,128)(2,1)} %fusion.19), channel_id=1, source_target_pairs={{31,0},{0,1},{1,2},{2,3},{3,4},{4,5},{5,6},{6,7},{7,8},{8,9},{9,10... | collective-permute-start | bytes 98312 | tf_op jit(solution)/shard_map/ppermute | solution.py:29
  103.5 2.3 %collective-permute-done.3 = bf16[1,1,32,128]{3,2,1,0:T(8,128)(2,1)S(1)} collective-permute-done((bf16[1,1,32,128]{3,2,1,0:T(8,128)(2,1)S(1)}, bf16[1,1,32,128]{3,2,1,0:T(8,128)(2,1)S(1)}, u32[]{:S(2)}, u32[]{:S(2)}) %collective-permute-start.3) | collective-permute-done | bytes 8224 | tf_op jit(solution)/shard_map/ppermute | solution.py:17
  105.8 0.9 maximum_bitcast_fusion.1
  106.7 1.8 %gather_fusion.1 = bf16[96,32,128]{2,1,0:T(8,128)(2,1)} fusion(bf16[18,32,128]{2,1,0:T(8,128)(2,1)S(1)} %maximum_bitcast_fusion.1, s32[1024]{0:T(1024)} %copy-done.8), kind=kCustom, calls=%fused_computation.1 | custom fusion | bytes 1573248 | tf_op jit(solution)/shard_map/gather | solution.py:57
  108.5 1.9 %collective-permute-done.5 = bf16[1,4,32,128]{3,2,1,0:T(8,128)(2,1)} collective-permute-done((bf16[1,4,32,128]{3,2,1,0:T(8,128)(2,1)}, bf16[1,4,32,128]{3,2,1,0:T(8,128)(2,1)}, u32[]{:S(2)}, u32[]{:S(2)}) %collective-permute-start.5) | collective-permute-done | bytes 32800 | tf_op jit(solution)/shard_map/ppermute | solution.py:29
  110.4 0.9 bitcast_add_fusion
  111.3 34.5 %all-to-all-done.1 = f32[16,1,16,32,128]{4,3,2,1,0:T(8,128)} async-done(((f32[16,1,16,32,128]{4,3,2,1,0:T(8,128)}), f32[16,1,16,32,128]{4,3,2,1,0:T(8,128)}, u32[]{:S(2)}, u32[]{:S(2)}) %all-to-all-start.1) | async-done | bytes 4194336 | tf_op jit(solution)/shard_map/all_to_all | solution.py:73
  145.8 6.5 %fusion = f32[1,16,32,128]{3,0,2,1:T(1,128)S(1)} fusion(f32[16,16,32,128]{3,2,1,0:T(8,128)} %bitcast.32, f32[16,16]{0,1:T(8,128)} %copy-done.13, s32[]{:T(128)S(6)} %select_n.31, pred[16,16]{0,1:T(8,128)(4,1)} %copy-done.15, s32[16,16]{0,1:T(8,128)} %copy-done.12), kind=kOutput, calls=%fused_computation.2 | convolution fusion | flops 12583056 | bytes 4457988 | tf_op jit(solution)/shard_map/jt,jnrc->tnrc/dot_general | solution.py:76
  152.4 1.4 multiply_add_fusion
  (57 shorter events, 0.5 us)
Async XLA Ops:
  0.0 79.4 %copy-start = (bf16[1,16,6,128,128]{4,3,2,1,0:T(8,128)(2,1)S(1)}, bf16[1,16,6,128,128]{4,3,2,1,0:T(8,128)(2,1)}, u32[]{:S(2)}) copy-start(bf16[1,16,6,128,128]{4,3,2,1,0:T(8,128)(2,1)} %param.13) | copy-start | bytes 9437188
  0.8 0.5 copy-start.16
  5.0 11.3 %copy-start.21 = (s32[1,4]{1,0:T(1,128)S(1)}, s32[1,4]{1,0:T(1,128)}, u32[]{:S(2)}) copy-start(s32[1,4]{1,0:T(1,128)} %param.16) | copy-start | bytes 52
  5.0 11.3 %copy-start.6 = (bf16[1,4,128,128]{3,2,1,0:T(8,128)(2,1)S(1)}, bf16[1,4,128,128]{3,2,1,0:T(8,128)(2,1)}, u32[]{:S(2)}) copy-start(bf16[1,4,128,128]{3,2,1,0:T(8,128)(2,1)} %param.14) | copy-start | bytes 393220
  5.0 25.2 %copy-start.18 = (s32[16,6]{0,1:T(8,128)S(1)}, s32[16,6]{0,1:T(8,128)}, u32[]{:S(2)}) copy-start(s32[16,6]{0,1:T(8,128)} %param.15) | copy-start | bytes 1156
  5.0 67.9 %all-to-all-start = ((f32[16,1,16,32,128]{4,3,2,1,0:T(8,128)}), f32[16,1,16,32,128]{4,3,2,1,0:T(8,128)}, u32[]{:S(2)}, u32[]{:S(2)}) async-start(f32[16,1,16,32,128]{4,3,2,1,0:T(8,128)} %stack.4), calls=%async_computation | async-start | bytes 8388608 | tf_op jit(solution)/shard_map/all_to_all | solution.py:73
  16.2 63.2 %copy-start.10 = (f32[1,16,128]{2,1,0:T(8,128)S(1)}, f32[1,16,128]{2,1,0:T(8,128)}, u32[]{:S(2)}) copy-start(f32[1,16,128]{2,1,0:T(8,128)} %param.11) | copy-start | bytes 24580
  16.3 13.9 %copy-start.19 = (f32[4]{0:T(128)}, f32[4]{0:T(128)S(1)}, u32[]{:S(2)}) copy-start(f32[4]{0:T(128)S(1)} %convert_bitcast_fusion) | copy-start | bytes 52
  17.1 21.8 %collective-permute-start.2 = (bf16[1,4,32,128]{3,2,1,0:T(8,128)(2,1)}, bf16[1,4,32,128]{3,2,1,0:T(8,128)(2,1)S(1)}, u32[]{:S(2)}, u32[]{:S(2)}) collective-permute-start(bf16[1,4,32,128]{3,2,1,0:T(8,128)(2,1)} %fusion.18), channel_id=1, source_target_pairs={{31,0},{0,1},{1,2},{2,3},{3,4},{4,5},{5,6},{6,7},{7,8},{8,9},{9,10... | collective-permute-start | bytes 98312 | tf_op jit(solution)/shard_map/ppermute | solution.py:29
  19.1 12.0 %collective-permute-start.1 = (bf16[1,1,32,128]{3,2,1,0:T(8,128)(2,1)S(1)}, bf16[1,1,32,128]{3,2,1,0:T(8,128)(2,1)S(1)}, u32[]{:S(2)}, u32[]{:S(2)}) collective-permute-start(bf16[1,1,32,128]{3,2,1,0:T(8,128)(2,1)S(1)} %get-tuple-element.12), channel_id=1, source_target_pairs={{1,0},{2,1},{3,2},{4,3},{5,4},{6,5},{7,6},{8,7},{9,8},{10,9},{11,1... | collective-permute-start | bytes 24584 | tf_op jit(solution)/shard_map/ppermute | solution.py:19
  28.2 8.3 %collective-permute-start = (bf16[1,1,32,128]{3,2,1,0:T(8,128)(2,1)S(1)}, bf16[1,1,32,128]{3,2,1,0:T(8,128)(2,1)}, u32[]{:S(2)}, u32[]{:S(2)}) collective-permute-start(bf16[1,1,32,128]{3,2,1,0:T(8,128)(2,1)S(1)} %get-tuple-element.11), channel_id=1, source_target_pairs={{0,1},{1,2},{2,3},{3,4},{4,5},{5,6},{6,7},{7,8},{8,9},{9,10},{10,1... | collective-permute-start | bytes 24584 | tf_op jit(solution)/shard_map/ppermute | solution.py:17
  30.4 49.0 %copy-start.8 = (s32[1024]{0:T(1024)}, s32[1024]{0:T(1024)S(1)}, u32[]{:S(2)}) copy-start(s32[1024]{0:T(1024)S(1)} %pad_clamp_fusion) | copy-start | bytes 12292
  30.4 49.0 %copy-start.12 = (s32[16,16]{0,1:T(8,128)}, s32[16,16]{0,1:T(8,128)S(1)}, u32[]{:S(2)}) copy-start(s32[16,16]{0,1:T(8,128)S(1)} %get-tuple-element.13) | copy-start | bytes 3076
  30.4 50.7 %copy-start.13 = (f32[16,16]{0,1:T(8,128)}, f32[16,16]{0,1:T(8,128)S(1)}, u32[]{:S(2)}) copy-start(f32[16,16]{0,1:T(8,128)S(1)} %get-tuple-element.14) | copy-start | bytes 3076
  31.0 48.4 %copy-start.15 = (pred[16,16]{0,1:T(8,128)(4,1)}, pred[16,16]{0,1:T(8,128)(4,1)S(1)}, u32[]{:S(2)}) copy-start(pred[16,16]{0,1:T(8,128)(4,1)S(1)} %fusion.21) | copy-start | bytes 772
  31.0 0.6 copy-start.14
  72.8 6.6 %copy-start.2 = (bf16[96,32,128]{2,1,0:T(8,128)(2,1)S(1)}, bf16[96,32,128]{2,1,0:T(8,128)(2,1)}, u32[]{:S(2)}) copy-start(bf16[96,32,128]{2,1,0:T(8,128)(2,1)} %gather_fusion) | copy-start | bytes 2359300
  72.8 6.6 %copy-start.7 = (f32[1,4,32,128]{3,2,1,0:T(8,128)S(1)}, f32[1,4,32,128]{3,2,1,0:T(8,128)}, u32[]{:S(2)}) copy-start(f32[1,4,32,128]{3,2,1,0:T(8,128)} %bitcast_add_fusion.1) | copy-start | bytes 196612
  72.8 8.3 %copy-start.9 = (f32[16,128]{1,0:T(8,128)S(1)}, f32[16,128]{1,0:T(8,128)}, u32[]{:S(2)}) copy-start(f32[16,128]{1,0:T(8,128)} %param.12) | copy-start | bytes 24580
  81.1 18.5 %copy-start.4 = (bf16[1,16,32,128]{3,2,1,0:T(8,128)(2,1)}, bf16[1,16,32,128]{3,2,1,0:T(8,128)(2,1)S(1)}, u32[]{:S(2)}) copy-start(bf16[1,16,32,128]{3,2,1,0:T(8,128)(2,1)S(1)} %get-tuple-element.5) | copy-start | bytes 393220
  83.8 16.9 %copy-start.20 = (f32[4]{0:T(128)S(1)}, f32[4]{0:T(128)}, u32[]{:S(2)}) copy-start(f32[4]{0:T(128)} %copy-done.19) | copy-start | bytes 52
  83.8 62.1 %all-to-all-start.1 = ((f32[16,1,16,32,128]{4,3,2,1,0:T(8,128)}), f32[16,1,16,32,128]{4,3,2,1,0:T(8,128)}, u32[]{:S(2)}, u32[]{:S(2)}) async-start(f32[16,1,16,32,128]{4,3,2,1,0:T(8,128)} %stack.5), calls=%async_computation.1 | async-start | bytes 8388608 | tf_op jit(solution)/shard_map/all_to_all | solution.py:73
  89.2 14.2 %collective-permute-start.4 = (bf16[1,1,32,128]{3,2,1,0:T(8,128)(2,1)S(1)}, bf16[1,1,32,128]{3,2,1,0:T(8,128)(2,1)S(1)}, u32[]{:S(2)}, u32[]{:S(2)}) collective-permute-start(bf16[1,1,32,128]{3,2,1,0:T(8,128)(2,1)S(1)} %get-tuple-element.10), channel_id=1, source_target_pairs={{1,0},{2,1},{3,2},{4,3},{5,4},{6,5},{7,6},{8,7},{9,8},{10,9},{11,1... | collective-permute-start | bytes 24584 | tf_op jit(solution)/shard_map/ppermute | solution.py:19
  97.7 8.1 %collective-permute-start.3 = (bf16[1,1,32,128]{3,2,1,0:T(8,128)(2,1)S(1)}, bf16[1,1,32,128]{3,2,1,0:T(8,128)(2,1)S(1)}, u32[]{:S(2)}, u32[]{:S(2)}) collective-permute-start(bf16[1,1,32,128]{3,2,1,0:T(8,128)(2,1)S(1)} %get-tuple-element.9), channel_id=1, source_target_pairs={{0,1},{1,2},{2,3},{3,4},{4,5},{5,6},{6,7},{7,8},{8,9},{9,10},{10,1... | collective-permute-start | bytes 24584 | tf_op jit(solution)/shard_map/ppermute | solution.py:17
  100.7 2.8 %copy-start.5 = (f32[4,32,128]{2,1,0:T(8,128)}, f32[4,32,128]{2,1,0:T(8,128)S(1)}, u32[]{:S(2)}) copy-start(f32[4,32,128]{2,1,0:T(8,128)S(1)} %fusion.14) | copy-start | bytes 196612
  101.4 9.0 %collective-permute-start.5 = (bf16[1,4,32,128]{3,2,1,0:T(8,128)(2,1)}, bf16[1,4,32,128]{3,2,1,0:T(8,128)(2,1)}, u32[]{:S(2)}, u32[]{:S(2)}) collective-permute-start(bf16[1,4,32,128]{3,2,1,0:T(8,128)(2,1)} %fusion.19), channel_id=1, source_target_pairs={{31,0},{0,1},{1,2},{2,3},{3,4},{4,5},{5,6},{6,7},{7,8},{8,9},{9,10... | collective-permute-start | bytes 98312 | tf_op jit(solution)/shard_map/ppermute | solution.py:29
  108.5 43.9 %copy-start.11 = (f32[1,16,128]{2,1,0:T(8,128)S(1)}, f32[1,16,128]{2,1,0:T(8,128)}, u32[]{:S(2)}) copy-start(f32[1,16,128]{2,1,0:T(8,128)} %param.11) | copy-start | bytes 24580
  108.5 43.9 %copy-start.17 = (f32[16]{0:T(128)S(1)}, f32[16]{0:T(128)}, u32[]{:S(2)}) copy-start(f32[16]{0:T(128)} %copy-done.16) | copy-start | bytes 196
  145.8 6.6 %copy-start.1 = (bf16[96,32,128]{2,1,0:T(8,128)(2,1)S(1)}, bf16[96,32,128]{2,1,0:T(8,128)(2,1)}, u32[]{:S(2)}) copy-start(bf16[96,32,128]{2,1,0:T(8,128)(2,1)} %gather_fusion.1) | copy-start | bytes 2359300
  145.8 6.6 %copy-start.3 = (f32[1,16,32,128]{3,2,1,0:T(8,128)S(1)}, f32[1,16,32,128]{3,2,1,0:T(8,128)}, u32[]{:S(2)}) copy-start(f32[1,16,32,128]{3,2,1,0:T(8,128)} %param.10) | copy-start | bytes 786436
